TPU v7x, 32 devices: a whole 2x2x4 slice. The times are simulated.
32 devices in a mesh: parts: 2 (over y), ctx: 4 (over z), head: 2 (over x), rep: 2 (over core).
Axes of the slice: x: 2, y: 2, z: 4, core: 2. Of those that a mesh axis runs over, the one named last changes fastest.
Arguments:
- query_rows: bfloat16 [4096, 8, 6, 128], P(('parts', 'ctx'), 'head', 'rep'), parts along dimension 0, may hold values from -125 to 125
- key_rows: bfloat16 [4096, 8, 128], P(('parts', 'ctx'), 'head'), parts along dimension 0, may hold values from -5 to 5
- value_rows: bfloat16 [4096, 8, 128], P(('parts', 'ctx'), 'head'), parts along dimension 0, may hold values from -6 to 6
- dest_block: int32 [32], P('parts'), parts along dimension 0, may hold values from 0 to 15, as said below
- tile_list: int32 [32, 4], P('parts'), parts along dimension 0, may hold values from 0 to 15, as said below
- tile_count: int32 [32], P('parts'), parts along dimension 0, may hold values from 1 to 4
- stripe_start: int32 [16, 4], P(('parts', 'head')), parts along dimension 0, may hold values from 0 to 1536, as said below
Outputs:
- attended: bfloat16 [4096, 8, 6, 128], P(('parts', 'ctx'), 'head', 'rep'), parts along dimension 0
There are 2 independent parts, one for each index of `parts`. A program takes and returns all parts, laid end to end along the dimension named above; each array names one. Nothing has to cross between parts.
Inputs may be any that keep to these rules, and one draw needn't show every extreme that they name: dest_block is a permutation of the blocks, so each index of ctx receives exactly 4 blocks (index of ctx of a position: dest_block // 4). For every ordered pair of indices of ctx, at most 1 of the first index's blocks take positions on the second, and some pair has exactly 1. tile_list[p, 0] == p; the 4 tiles of a row are distinct and all on the same index of ctx as p (tile_list[p, j] // 4 == p // 4). Each stripe lies in the rows of one index of ctx: stripe_start // 512 == (stripe_start + 511) // 512 (since a stripe is 512 keys long, stripe_start is a multiple of 512).
All inputs are finite; a program needn't handle non-finite values.
Results may differ from a plain program's by a relative error of at most 0.0048.
Values may be sent and summed in bfloat16 or wider, within the bound.
No kernel may reach another device: no remote copies, remote signals or barrier semaphores. Data moves between devices by JAX's collectives and lax.ppermute only.
A program may use at most 64 MiB of HBM per device.

v0:
```python
import jax
import jax.numpy as jnp
from jax import lax
from jax.sharding import PartitionSpec as P

STRIPE = 512


def attend(query_block, tile_key, tile_value, tile_used, stripe_keys, stripe_values):
    scaling = query_block.shape[-1] ** (-0.5)
    block_rows = query_block.shape[0]
    near_scores = (
        jnp.einsum("qhgd,khd->hgqk", query_block, tile_key, preferred_element_type=jnp.float32)
        * scaling
    )
    far_scores = (
        jnp.einsum("qhgd,hkd->hgqk", query_block, stripe_keys, preferred_element_type=jnp.float32)
        * scaling
    )
    kept_mask = jnp.arange(near_scores.shape[-1], dtype=jnp.int32) // block_rows < tile_used
    near_scores = jnp.where(kept_mask, near_scores, -1e30)
    row_top = jnp.maximum(jnp.max(near_scores, axis=-1), jnp.max(far_scores, axis=-1))[..., None]
    near_weight = jnp.exp(near_scores - row_top)
    far_weight = jnp.exp(far_scores - row_top)
    denominator = jnp.sum(near_weight, axis=-1) + jnp.sum(far_weight, axis=-1)
    summed = jnp.einsum(
        "hgqk,khd->qhgd",
        near_weight.astype(jnp.bfloat16),
        tile_value,
        preferred_element_type=jnp.float32,
    )
    summed = summed + jnp.einsum(
        "hgqk,hkd->qhgd",
        far_weight.astype(jnp.bfloat16),
        stripe_values,
        preferred_element_type=jnp.float32,
    )
    return (summed / jnp.transpose(denominator, (2, 0, 1))[..., None]).astype(jnp.bfloat16)


def attend_all(
    query_blocks, tile_ids, counts, key_blocks, value_blocks, stripe_keys, stripe_values
):
    head_local = key_blocks.shape[2]
    head_width = key_blocks.shape[3]

    def attend_block(packed):
        query_block, tile_row, tile_used = packed
        tile_key = key_blocks[tile_row].reshape(-1, head_local, head_width)
        tile_value = value_blocks[tile_row].reshape(-1, head_local, head_width)
        return attend(query_block, tile_key, tile_value, tile_used, stripe_keys, stripe_values)

    return lax.map(attend_block, (query_blocks, tile_ids, counts))


def local(query_rows, key_rows, value_rows, dest_block, tile_list, tile_count, stripe_start):
    device_count = lax.axis_size("ctx")
    ctx_index = lax.axis_index("ctx")
    tok_rows, head_local, group_local, head_width = query_rows.shape
    block_total = dest_block.shape[0]
    per_device = block_total // device_count
    block_rows = tok_rows // per_device
    stripe_count = stripe_start.shape[1]
    capacity = max(1, per_device // device_count)
    block_index = jnp.arange(block_total, dtype=jnp.int32)
    inverse = jnp.zeros((block_total,), jnp.int32).at[dest_block].set(block_index)
    local_index = jnp.arange(per_device, dtype=jnp.int32)
    own_ids = ctx_index * per_device + local_index
    owner_dev = (dest_block // per_device).reshape(device_count, per_device)
    earlier = local_index[:, None] > local_index[None, :]
    same_dest = owner_dev[:, :, None] == owner_dev[:, None, :]
    rank_table = jnp.sum((same_dest & earlier[None]).astype(jnp.int32), axis=2)
    send_slots = owner_dev * capacity + rank_table
    own_slots = send_slots[ctx_index]
    slot_range = jnp.arange(device_count * capacity, dtype=jnp.int32)
    slot_source = jnp.sum(
        jnp.where(own_slots[:, None] == slot_range[None, :], local_index[:, None], 0), axis=0
    )
    query_flat = query_rows.reshape(per_device, block_rows, head_local * group_local * head_width)
    key_flat = key_rows.reshape(per_device, block_rows, head_local * head_width)
    value_flat = value_rows.reshape(per_device, block_rows, head_local * head_width)
    arrived = (
        lax.all_to_all(query_flat[slot_source], "ctx", split_axis=0, concat_axis=0, tiled=True),
        lax.all_to_all(key_flat[slot_source], "ctx", split_axis=0, concat_axis=0, tiled=True),
        lax.all_to_all(value_flat[slot_source], "ctx", split_axis=0, concat_axis=0, tiled=True),
    )
    anchor = inverse[own_ids]
    arrive_slot = (
        anchor // per_device * capacity + rank_table[anchor // per_device, anchor % per_device]
    )
    query_new = arrived[0][arrive_slot].reshape(
        per_device, block_rows, head_local, group_local, head_width
    )
    key_new = arrived[1][arrive_slot].reshape(tok_rows, head_local, head_width)
    value_new = arrived[2][arrive_slot].reshape(tok_rows, head_local, head_width)
    stripe_first = stripe_start.reshape(-1)
    stripe_head = jnp.arange(stripe_first.shape[0], dtype=jnp.int32) // stripe_count

    def cut_stripe(head_id, first_row):
        offset = first_row % tok_rows
        key_head = lax.dynamic_index_in_dim(key_new, head_id, 1, keepdims=False)
        value_head = lax.dynamic_index_in_dim(value_new, head_id, 1, keepdims=False)
        return jnp.stack([key_head, value_head])

    pieces = jax.vmap(cut_stripe)(stripe_head, stripe_first)
    owned = (stripe_first // tok_rows == ctx_index)[:, None, None, None]
    owned_terms = jnp.where(owned, pieces, jnp.zeros((), jnp.bfloat16))
    stacked = lax.psum(owned_terms, "ctx").astype(jnp.float32).astype(jnp.bfloat16)
    stripe_keys = stacked[:, 0].reshape(head_local, stripe_count * STRIPE, head_width)
    stripe_values = stacked[:, 1].reshape(head_local, stripe_count * STRIPE, head_width)
    tiles_new = tile_list[own_ids] - ctx_index * per_device
    counts = tile_count[own_ids]
    key_blocks = key_new.reshape(per_device, block_rows, head_local, head_width)
    value_blocks = value_new.reshape(per_device, block_rows, head_local, head_width)
    out_new = attend_all(
        query_new, tiles_new, counts, key_blocks, value_blocks, stripe_keys, stripe_values
    )
    return_source = jnp.sum(
        jnp.where(arrive_slot[:, None] == slot_range[None, :], local_index[:, None], 0), axis=0
    )
    returned = lax.all_to_all(
        out_new.reshape(per_device, block_rows, -1)[return_source],
        "ctx",
        split_axis=0,
        concat_axis=0,
        tiled=True,
    )
    result = returned[own_slots].reshape(query_rows.shape)
    return result


def solution(mesh):
    in_specs = (
        P(("parts", "ctx"), "head", "rep", None),
        P(("parts", "ctx"), "head", None),
        P(("parts", "ctx"), "head", None),
        P("parts"),
        P("parts", None),
        P("parts"),
        P(("parts", "head"), None),
    )
    out_specs = P(("parts", "ctx"), "head", "rep", None)
    return jax.shard_map(local, mesh=mesh, in_specs=in_specs, out_specs=out_specs, check_vma=False)
```

profile of v0, /device:TPU:0, one launch (start us, length us, event | category | flops | bytes accessed | tf_op | source)
XLA Modules:
  0.0 429.6 jit_solution(15590666713226647487)
XLA Ops:
  10.3 6.3 %all-to-all-start.1 = ((bf16[4,128,512]{2,1,0:T(8,128)(2,1)}), bf16[4,128,512]{2,1,0:T(8,128)(2,1)S(1)}, u32[]{:S(2)}, u32[]{:S(2)}) async-start(bf16[4,128,512]{2,1,0:T(8,128)(2,1)} %gather_fusion.8), calls=%async_computation.1 | async-start | bytes 1048576 | tf_op jit(solution)/shard_map/all_to_all | solution.py:84
  19.6 11.6 %all-to-all-done.1 = bf16[4,128,512]{2,1,0:T(8,128)(2,1)S(1)} async-done(((bf16[4,128,512]{2,1,0:T(8,128)(2,1)}), bf16[4,128,512]{2,1,0:T(8,128)(2,1)S(1)}, u32[]{:S(2)}, u32[]{:S(2)}) %all-to-all-start.1) | async-done | bytes 524320 | tf_op jit(solution)/shard_map/all_to_all | solution.py:84
  31.2 3.5 all-to-all-start
  37.3 11.3 %all-to-all-done = bf16[4,128,512]{2,1,0:T(8,128)(2,1)S(1)} async-done(((bf16[4,128,512]{2,1,0:T(8,128)(2,1)}), bf16[4,128,512]{2,1,0:T(8,128)(2,1)S(1)}, u32[]{:S(2)}, u32[]{:S(2)}) %all-to-all-start) | async-done | bytes 524320 | tf_op jit(solution)/shard_map/all_to_all | solution.py:85
  53.2 3.5 fusion.60
  61.8 3.4 gather_fusion.10
  65.2 3.9 all-to-all-start.2
  72.4 74.7 %all-to-all-done.2 = bf16[4,128,1536]{2,1,0:T(8,128)(2,1)S(1)} async-done(((bf16[4,128,1536]{2,1,0:T(8,128)(2,1)}), bf16[4,128,1536]{2,1,0:T(8,128)(2,1)S(1)}, u32[]{:S(2)}, u32[]{:S(2)}) %all-to-all-start.2) | async-done | bytes 1572896 | tf_op jit(solution)/shard_map/all_to_all | solution.py:83
  149.3 95.1 %all-reduce.2.cloned.1.call-done = bf16[16,2,512,128]{2,3,0,1:T(8,128)(2,1)} async-done(((bf16[16,2,512,128]{2,3,0,1:T(8,128)(2,1)}), bf16[16,2,512,128]{2,3,0,1:T(8,128)(2,1)}) %all-reduce.2.cloned.1.call-update) | async-done | bytes 4194320 | tf_op jit(solution)/shard_map/psum | solution.py:108
  244.4 3.9 fusion.80
  248.3 3.9 copy.85
  254.6 115.6 %while.12 = (s32[]{:T(128)}, bf16[4,128,4,3,128]{1,4,3,2,0:T(8,128)(2,1)}, s32[4,4]{1,0:T(4,128)S(1)}, bf16[4,128,4,128]{3,2,1,0:T(4,128)(2,1)}, s32[4]{0:T(128)...) while((s32[]{:T(128)}, ...), condition=%wide.region_9.10_spmd, body=%wide.region_4.9_spmd.sunk | while | flops 2047674880 | bytes 124487448 | solution.py:53
  254.6 2.8 gather_fusion
  260.5 3.0 bitcast_reduce_fusion.4
  269.6 8.0 %fusion.97 = f32[128,4,3,128]{0,3,2,1:T(8,128)} fusion(bf16[4,2048,128]{2,1,0:T(8,128)(2,1)S(1)} %copy-done.3, f32[4,128,3,2048]{3,1,2,0:T(8,128)} %copy-done.2, f32[4,3,128]{2,1,0:T(4,128)S(1)} %max.11), kind=kOutput, calls=%fused_computation.39.clone.1 | convolution fusion | flops 814743552 | bytes 15472640 | tf_op jit(solution)/shard_map/while/body/eval_jaxpr/hgqk,hkd->qhgd/dot_general | solution.py:32
  280.5 3.1 fusion.100
  283.5 2.8 gather_fusion
  289.4 3.0 bitcast_reduce_fusion.4
  298.5 8.0 %fusion.97 = f32[128,4,3,128]{0,3,2,1:T(8,128)} fusion(bf16[4,2048,128]{2,1,0:T(8,128)(2,1)S(1)} %copy-done.3, f32[4,128,3,2048]{3,1,2,0:T(8,128)} %copy-done.2, f32[4,3,128]{2,1,0:T(4,128)S(1)} %max.11), kind=kOutput, calls=%fused_computation.39.clone.1 | convolution fusion | flops 814743552 | bytes 15472640 | tf_op jit(solution)/shard_map/while/body/eval_jaxpr/hgqk,hkd->qhgd/dot_general | solution.py:32
  309.4 3.1 fusion.100
  312.4 2.8 gather_fusion
  318.3 3.0 bitcast_reduce_fusion.4
  327.5 8.0 %fusion.97 = f32[128,4,3,128]{0,3,2,1:T(8,128)} fusion(bf16[4,2048,128]{2,1,0:T(8,128)(2,1)S(1)} %copy-done.3, f32[4,128,3,2048]{3,1,2,0:T(8,128)} %copy-done.2, f32[4,3,128]{2,1,0:T(4,128)S(1)} %max.11), kind=kOutput, calls=%fused_computation.39.clone.1 | convolution fusion | flops 814743552 | bytes 15472640 | tf_op jit(solution)/shard_map/while/body/eval_jaxpr/hgqk,hkd->qhgd/dot_general | solution.py:32
  335.5 2.8 gather_fusion.1
  338.3 3.1 fusion.100
  341.3 2.8 gather_fusion
  347.2 3.0 bitcast_reduce_fusion.4
  356.4 8.0 %fusion.97 = f32[128,4,3,128]{0,3,2,1:T(8,128)} fusion(bf16[4,2048,128]{2,1,0:T(8,128)(2,1)S(1)} %copy-done.3, f32[4,128,3,2048]{3,1,2,0:T(8,128)} %copy-done.2, f32[4,3,128]{2,1,0:T(4,128)S(1)} %max.11), kind=kOutput, calls=%fused_computation.39.clone.1 | convolution fusion | flops 814743552 | bytes 15472640 | tf_op jit(solution)/shard_map/while/body/eval_jaxpr/hgqk,hkd->qhgd/dot_general | solution.py:32
  367.2 3.1 fusion.100
  373.7 3.6 all-to-all-start.3
  377.4 37.0 %all-to-all-done.3 = bf16[4,128,1536]{2,1,0:T(8,128)(2,1)S(1)} async-done(((bf16[4,128,1536]{2,1,0:T(8,128)(2,1)}), bf16[4,128,1536]{2,1,0:T(8,128)(2,1)S(1)}, u32[]{:S(2)}, u32[]{:S(2)}) %all-to-all-start.3) | async-done | bytes 1572896 | tf_op jit(solution)/shard_map/all_to_all | solution.py:121
  416.1 4.6 %reshape.508 = bf16[512,4,3,128]{3,2,1,0:T(4,128)(2,1)S(1)} reshape(bf16[4,128,1536]{2,1,0:T(8,128)(2,1)} %gather_fusion.15) | data formatting | bytes 3145728 | tf_op jit(solution)/shard_map/reshape | solution.py:128
  (138 shorter events, 79.1 us)
Async XLA Ops:
  6.5 63.2 %copy-start = (s32[16]{0:T(128)S(1)}, s32[16]{0:T(128)}, u32[]{:S(2)}) copy-start(s32[16]{0:T(128)} %param.14) | copy-start | bytes 196
  6.5 10.1 %copy-start.9 = (bf16[512,4,128]{2,1,0:T(4,128)(2,1)S(1)}, bf16[512,4,128]{2,1,0:T(4,128)(2,1)}, u32[]{:S(2)}) copy-start(bf16[512,4,128]{2,1,0:T(4,128)(2,1)} %param.11) | copy-start | bytes 1572868
  10.3 20.8 %all-to-all-start.1 = ((bf16[4,128,512]{2,1,0:T(8,128)(2,1)}), bf16[4,128,512]{2,1,0:T(8,128)(2,1)S(1)}, u32[]{:S(2)}, u32[]{:S(2)}) async-start(bf16[4,128,512]{2,1,0:T(8,128)(2,1)} %gather_fusion.8), calls=%async_computation.1 | async-start | bytes 1048576 | tf_op jit(solution)/shard_map/all_to_all | solution.py:84
  16.7 18.7 %copy-start.11 = (s32[4,4]{1,0:T(4,128)S(1)}, s32[4,4]{1,0:T(4,128)}, u32[]{:S(2)}) copy-start(s32[4,4]{1,0:T(4,128)} %param.15) | copy-start | bytes 196
  31.2 17.5 %all-to-all-start = ((bf16[4,128,512]{2,1,0:T(8,128)(2,1)}), bf16[4,128,512]{2,1,0:T(8,128)(2,1)S(1)}, u32[]{:S(2)}, u32[]{:S(2)}) async-start(bf16[4,128,512]{2,1,0:T(8,128)(2,1)} %gather_fusion.3), calls=%async_computation | async-start | bytes 1048576 | tf_op jit(solution)/shard_map/all_to_all | solution.py:85
  34.6 209.7 %all-reduce.2.cloned.1.call-start = ((), (), s32[]{:S(2)}) async-start(), calls=%async_computation.4 | async-start | bytes 8388608 | tf_op jit(solution)/shard_map/psum | solution.py:108
  36.1 0.8 copy-start.5
  49.2 0.8 copy-start.7
  65.2 3.9 copy-start.10
  65.2 5.3 %copy-start.8 = (bf16[4,128,512]{2,1,0:T(8,128)(2,1)S(1)}, bf16[4,128,512]{2,1,0:T(8,128)(2,1)}, u32[]{:S(2)}) copy-start(bf16[4,128,512]{2,1,0:T(8,128)(2,1)} %copy-done.7) | copy-start | bytes 1572868
  65.2 6.3 %copy-start.6 = (bf16[4,128,512]{2,1,0:T(8,128)(2,1)S(1)}, bf16[4,128,512]{2,1,0:T(8,128)(2,1)}, u32[]{:S(2)}) copy-start(bf16[4,128,512]{2,1,0:T(8,128)(2,1)} %copy-done.5) | copy-start | bytes 1572868
  65.2 81.9 %all-to-all-start.2 = ((bf16[4,128,1536]{2,1,0:T(8,128)(2,1)}), bf16[4,128,1536]{2,1,0:T(8,128)(2,1)S(1)}, u32[]{:S(2)}, u32[]{:S(2)}) async-start(bf16[4,128,1536]{2,1,0:T(8,128)(2,1)} %gather_fusion.10), calls=%async_computation.2 | async-start | bytes 3145728 | tf_op jit(solution)/shard_map/all_to_all | solution.py:83
  257.4 3.1 copy-start.4
  263.5 4.6 %copy-start.2 = (f32[4,128,3,2048]{3,1,2,0:T(8,128)}, f32[4,128,3,2048]{3,1,2,0:T(8,128)S(1)}, u32[]{:S(2)}) copy-start(f32[4,128,3,2048]{3,1,2,0:T(8,128)S(1)} %get-tuple-element.250) | copy-start | bytes 37748740 | tf_op jit(solution)/shard_map/while
  268.1 1.6 copy-start.3
  286.3 3.1 copy-start.4
  292.4 4.6 %copy-start.2 = (f32[4,128,3,2048]{3,1,2,0:T(8,128)}, f32[4,128,3,2048]{3,1,2,0:T(8,128)S(1)}, u32[]{:S(2)}) copy-start(f32[4,128,3,2048]{3,1,2,0:T(8,128)S(1)} %get-tuple-element.250) | copy-start | bytes 37748740 | tf_op jit(solution)/shard_map/while
  297.0 1.6 copy-start.3
  315.2 3.1 copy-start.4
  321.3 4.6 %copy-start.2 = (f32[4,128,3,2048]{3,1,2,0:T(8,128)}, f32[4,128,3,2048]{3,1,2,0:T(8,128)S(1)}, u32[]{:S(2)}) copy-start(f32[4,128,3,2048]{3,1,2,0:T(8,128)S(1)} %get-tuple-element.250) | copy-start | bytes 37748740 | tf_op jit(solution)/shard_map/while
  325.9 1.6 copy-start.3
  344.1 3.1 copy-start.4
  350.2 4.6 %copy-start.2 = (f32[4,128,3,2048]{3,1,2,0:T(8,128)}, f32[4,128,3,2048]{3,1,2,0:T(8,128)S(1)}, u32[]{:S(2)}) copy-start(f32[4,128,3,2048]{3,1,2,0:T(8,128)S(1)} %get-tuple-element.250) | copy-start | bytes 37748740 | tf_op jit(solution)/shard_map/while
  354.8 1.6 copy-start.3
  373.7 40.6 %all-to-all-start.3 = ((bf16[4,128,1536]{2,1,0:T(8,128)(2,1)}), bf16[4,128,1536]{2,1,0:T(8,128)(2,1)S(1)}, u32[]{:S(2)}, u32[]{:S(2)}) async-start(bf16[4,128,1536]{2,1,0:T(8,128)(2,1)} %gather_fusion.14), calls=%async_computation.3 | async-start | bytes 3145728 | tf_op jit(solution)/shard_map/all_to_all | solution.py:121
  416.1 6.6 %copy-start.1 = (s32[16]{0:T(128)S(1)}, s32[16]{0:T(128)}, u32[]{:S(2)}) copy-start(s32[16]{0:T(128)} %param.14) | copy-start | bytes 196
Sparse Core Ops, SparseCore 0:
  56.9 187.4 all-reduce.1
where the time goes:
time: 431 us; the launch traced here: 430 us
  waiting for transfers between devices  230 us (53%)
  local copies, waits for them, and re-layouts  85 us (20%)
  matrix products  63.5 us (15%)
  other arithmetic  20.2 us (5%)
  starting transfers between devices  17.3 us (4%)
  between operations  13.7 us (3%)
    psum x1, waiting for transfers between devices, local(): lax.psum(owned_terms, 'ctx').astype(jnp.float32).astype(jnp.bfloat16)  95.1 us
    all_to_all x1, waiting for transfers between devices, local(): lax.all_to_all(query_flat[slot_source], 'ctx', split_axis=0, concat_axis=...  74.7 us
    all_to_all x1, waiting for transfers between devices, local(): lax.all_to_all(out_new.reshape(per_device, block_rows, -1)[return_source]...  37 us
    dot_general x4, matrix products, attend(): jnp.einsum('hgqk,hkd->qhgd', far_weight.astype(jnp.bfloat16), stripe_valu...  32.1 us
    reduce_sum x8, other arithmetic, attend(): denominator = jnp.sum(near_weight, axis=-1) + jnp.sum(far_weight, axis=-1)  12.7 us
    dot_general x4, matrix products, attend(): jnp.einsum('hgqk,khd->qhgd', near_weight.astype(jnp.bfloat16), tile_value...  12.2 us
    dot_general x4, matrix products, attend(): jnp.einsum('qhgd,hkd->hgqk', query_block, stripe_keys, preferred_element_...  12 us
    while x24, local copies, waits for them, and re-layouts  11.8 us
  transfers between devices with their start and end apart: 5, of which 5 were waited for; matrix products, arithmetic and copies ran while one was open for 4% of the time, Pallas kernels for 0%

commit v1 on v0

--- a/solution.py
+++ b/solution.py
@@ -105,7 +105,9 @@
     pieces = jax.vmap(cut_stripe)(stripe_head, stripe_first)
     owned = (stripe_first // tok_rows == ctx_index)[:, None, None, None]
     owned_terms = jnp.where(owned, pieces, jnp.zeros((), jnp.bfloat16))
-    stacked = lax.psum(owned_terms, "ctx").astype(jnp.float32).astype(jnp.bfloat16)
+    stacked = (
+        jnp.sum(lax.all_gather(owned_terms, "ctx"), axis=0).astype(jnp.float32).astype(jnp.bfloat16)
+    )
     stripe_keys = stacked[:, 0].reshape(head_local, stripe_count * STRIPE, head_width)
     stripe_values = stacked[:, 1].reshape(head_local, stripe_count * STRIPE, head_width)
     tiles_new = tile_list[own_ids] - ctx_index * per_device

time: 431 us -> 575 us (1.33)
  waiting for transfers between devices: 230 us -> 361 us
  other arithmetic: 20.2 us -> 31.9 us
    all_gather x0 -> x1, waiting for transfers between devices: none -> 217 us  [local(): lax.all_gather(owned_terms, 'ctx')]
    psum x1 -> x0, waiting for transfers between devices: 95.1 us -> none  [local(): lax.psum(owned_terms, 'ctx').astype(jnp.float32).astype(jnp.bfloat16)]
    reduce_sum x0 -> x1, other arithmetic: none -> 11.8 us  [local(): jnp.sum(lax.all_gather(owned_terms, 'ctx'), axis=0).astype(jnp.float32)]
    all_to_all x1, waiting for transfers between devices: 74.7 us -> 83.5 us  [local(): lax.all_to_all(query_flat[slot_source], 'ctx', split_axis=0, concat_axis=...]
  transfers between devices with their start and end apart: 5 -> 5, of which waited for: 5 -> 5; matrix products, arithmetic and copies ran while one was open for 4% -> 3% of each run, Pallas kernels for 0% -> 0%
where the time goes in v1:
time: 575 us; the launch traced here: 573 us
  waiting for transfers between devices  361 us (63%)
  local copies, waits for them, and re-layouts  85.4 us (15%)
  matrix products  63.6 us (11%)
  other arithmetic  31.9 us (6%)
  starting transfers between devices  17.3 us (3%)
  between operations  13.7 us (2%)
    all_gather x1, waiting for transfers between devices, local(): lax.all_gather(owned_terms, 'ctx')  217 us
    all_to_all x1, waiting for transfers between devices, local(): lax.all_to_all(query_flat[slot_source], 'ctx', split_axis=0, concat_axis=...  83.5 us
    all_to_all x1, waiting for transfers between devices, local(): lax.all_to_all(out_new.reshape(per_device, block_rows, -1)[return_source]...  37.4 us
    dot_general x4, matrix products, attend(): jnp.einsum('hgqk,hkd->qhgd', far_weight.astype(jnp.bfloat16), stripe_valu...  32.2 us
    reduce_sum x8, other arithmetic, attend(): denominator = jnp.sum(near_weight, axis=-1) + jnp.sum(far_weight, axis=-1)  12.7 us
    dot_general x4, matrix products, attend(): jnp.einsum('hgqk,khd->qhgd', near_weight.astype(jnp.bfloat16), tile_value...  12.2 us
    dot_general x4, matrix products, attend(): jnp.einsum('qhgd,hkd->hgqk', query_block, stripe_keys, preferred_element_...  12 us
    reduce_sum x1, other arithmetic, local(): jnp.sum(lax.all_gather(owned_terms, 'ctx'), axis=0).astype(jnp.float32)  11.8 us
  transfers between devices with their start and end apart: 5, of which 5 were waited for; matrix products, arithmetic and copies ran while one was open for 3% of the time, Pallas kernels for 0%

profile of v1, /device:TPU:0, one launch (start us, length us, event | category | flops | bytes accessed | tf_op | source)
XLA Modules:
  0.0 573.2 jit_solution(651617207816832597)
XLA Ops:
  10.3 6.3 %all-to-all-start.1 = ((bf16[4,128,512]{2,1,0:T(8,128)(2,1)}), bf16[4,128,512]{2,1,0:T(8,128)(2,1)S(1)}, u32[]{:S(2)}, u32[]{:S(2)}) async-start(bf16[4,128,512]{2,1,0:T(8,128)(2,1)} %gather_fusion.8), calls=%async_computation.1 | async-start | bytes 1048576 | tf_op jit(solution)/shard_map/all_to_all | solution.py:84
  19.6 11.6 %all-to-all-done.1 = bf16[4,128,512]{2,1,0:T(8,128)(2,1)S(1)} async-done(((bf16[4,128,512]{2,1,0:T(8,128)(2,1)}), bf16[4,128,512]{2,1,0:T(8,128)(2,1)S(1)}, u32[]{:S(2)}, u32[]{:S(2)}) %all-to-all-start.1) | async-done | bytes 524320 | tf_op jit(solution)/shard_map/all_to_all | solution.py:84
  31.2 3.5 all-to-all-start
  37.4 11.3 %all-to-all-done = bf16[4,128,512]{2,1,0:T(8,128)(2,1)S(1)} async-done(((bf16[4,128,512]{2,1,0:T(8,128)(2,1)}), bf16[4,128,512]{2,1,0:T(8,128)(2,1)S(1)}, u32[]{:S(2)}, u32[]{:S(2)}) %all-to-all-start) | async-done | bytes 524320 | tf_op jit(solution)/shard_map/all_to_all | solution.py:85
  53.2 3.4 fusion.60
  61.7 3.5 gather_fusion.10
  65.2 3.9 all-to-all-start.2
  72.4 83.5 %all-to-all-done.2 = bf16[4,128,1536]{2,1,0:T(8,128)(2,1)S(1)} async-done(((bf16[4,128,1536]{2,1,0:T(8,128)(2,1)}), bf16[4,128,1536]{2,1,0:T(8,128)(2,1)S(1)}, u32[]{:S(2)}, u32[]{:S(2)}) %all-to-all-start.2) | async-done | bytes 1572896 | tf_op jit(solution)/shard_map/all_to_all | solution.py:83
  158.2 217.5 %all-gather.3.cloned.1.call-done = bf16[64,2,512,128]{2,3,0,1:T(8,128)(2,1)} async-done(((bf16[16,2,512,128]{2,3,0,1:T(8,128)(2,1)}), bf16[64,2,512,128]{2,3,0,1:T(8,128)(2,1)}) %all-gather.3.cloned.1.call-update) | async-done | bytes 16777232 | tf_op jit(solution)/shard_map/all_gather | solution.py:109
  375.6 11.8 %reduce_sum.70 = bf16[16,2,512,128]{2,3,0,1:T(8,128)(2,1)} reduce(bf16[4,16,2,512,128]{3,4,1,0,2:T(8,128)(2,1)} %bitcast.190, bf16[]{:T(256)} %constant.146.clone.1), dimensions={0}, to_apply=%region_3.4 | reduce | flops 6291456 | bytes 20971522 | tf_op jit(solution)/shard_map/reduce_sum | solution.py:109
  387.5 3.9 fusion.80
  391.4 3.9 copy.107
  397.7 115.9 %while.12 = (s32[]{:T(128)}, bf16[4,128,4,3,128]{1,4,3,2,0:T(8,128)(2,1)}, s32[4,4]{1,0:T(4,128)S(1)}, bf16[4,128,4,128]{3,2,1,0:T(4,128)(2,1)}, s32[4]{0:T(128)...) while((s32[]{:T(128)}, ...), condition=%wide.region_9.10_spmd, body=%wide.region_4.9_spmd.sunk | while | flops 2047674880 | bytes 124487448 | solution.py:53
  403.6 3.0 bitcast_reduce_fusion.4
  412.8 8.0 %fusion.97 = f32[128,4,3,128]{0,3,2,1:T(8,128)} fusion(bf16[4,2048,128]{2,1,0:T(8,128)(2,1)S(1)} %copy-done.3, f32[4,128,3,2048]{3,1,2,0:T(8,128)} %copy-done.2, f32[4,3,128]{2,1,0:T(4,128)S(1)} %max.11), kind=kOutput, calls=%fused_computation.39.clone.1 | convolution fusion | flops 814743552 | bytes 15472640 | tf_op jit(solution)/shard_map/while/body/eval_jaxpr/hgqk,hkd->qhgd/dot_general | solution.py:32
  420.8 2.8 gather_fusion.1
  423.6 3.1 fusion.100
  432.6 3.0 bitcast_reduce_fusion.4
  441.7 8.0 %fusion.97 = f32[128,4,3,128]{0,3,2,1:T(8,128)} fusion(bf16[4,2048,128]{2,1,0:T(8,128)(2,1)S(1)} %copy-done.3, f32[4,128,3,2048]{3,1,2,0:T(8,128)} %copy-done.2, f32[4,3,128]{2,1,0:T(4,128)S(1)} %max.11), kind=kOutput, calls=%fused_computation.39.clone.1 | convolution fusion | flops 814743552 | bytes 15472640 | tf_op jit(solution)/shard_map/while/body/eval_jaxpr/hgqk,hkd->qhgd/dot_general | solution.py:32
  449.8 2.8 gather_fusion.1
  452.6 3.1 fusion.100
  461.6 3.0 bitcast_reduce_fusion.4
  470.7 8.0 %fusion.97 = f32[128,4,3,128]{0,3,2,1:T(8,128)} fusion(bf16[4,2048,128]{2,1,0:T(8,128)(2,1)S(1)} %copy-done.3, f32[4,128,3,2048]{3,1,2,0:T(8,128)} %copy-done.2, f32[4,3,128]{2,1,0:T(4,128)S(1)} %max.11), kind=kOutput, calls=%fused_computation.39.clone.1 | convolution fusion | flops 814743552 | bytes 15472640 | tf_op jit(solution)/shard_map/while/body/eval_jaxpr/hgqk,hkd->qhgd/dot_general | solution.py:32
  478.7 2.8 gather_fusion.1
  481.5 3.1 fusion.100
  490.5 3.0 bitcast_reduce_fusion.4
  499.7 8.0 %fusion.97 = f32[128,4,3,128]{0,3,2,1:T(8,128)} fusion(bf16[4,2048,128]{2,1,0:T(8,128)(2,1)S(1)} %copy-done.3, f32[4,128,3,2048]{3,1,2,0:T(8,128)} %copy-done.2, f32[4,3,128]{2,1,0:T(4,128)S(1)} %max.11), kind=kOutput, calls=%fused_computation.39.clone.1 | convolution fusion | flops 814743552 | bytes 15472640 | tf_op jit(solution)/shard_map/while/body/eval_jaxpr/hgqk,hkd->qhgd/dot_general | solution.py:32
  507.7 2.8 gather_fusion.1
  510.5 3.1 fusion.100
  517.1 3.6 all-to-all-start.3
  520.7 37.4 %all-to-all-done.3 = bf16[4,128,1536]{2,1,0:T(8,128)(2,1)S(1)} async-done(((bf16[4,128,1536]{2,1,0:T(8,128)(2,1)}), bf16[4,128,1536]{2,1,0:T(8,128)(2,1)S(1)}, u32[]{:S(2)}, u32[]{:S(2)}) %all-to-all-start.3) | async-done | bytes 1572896 | tf_op jit(solution)/shard_map/all_to_all | solution.py:123
  559.8 4.6 reshape.509
  (139 shorter events, 82.1 us)
Async XLA Ops:
  6.5 63.2 %copy-start = (s32[16]{0:T(128)S(1)}, s32[16]{0:T(128)}, u32[]{:S(2)}) copy-start(s32[16]{0:T(128)} %param.14) | copy-start | bytes 196
  6.5 10.1 %copy-start.9 = (bf16[512,4,128]{2,1,0:T(4,128)(2,1)S(1)}, bf16[512,4,128]{2,1,0:T(4,128)(2,1)}, u32[]{:S(2)}) copy-start(bf16[512,4,128]{2,1,0:T(4,128)(2,1)} %param.11) | copy-start | bytes 1572868
  10.3 20.8 %all-to-all-start.1 = ((bf16[4,128,512]{2,1,0:T(8,128)(2,1)}), bf16[4,128,512]{2,1,0:T(8,128)(2,1)S(1)}, u32[]{:S(2)}, u32[]{:S(2)}) async-start(bf16[4,128,512]{2,1,0:T(8,128)(2,1)} %gather_fusion.8), calls=%async_computation.1 | async-start | bytes 1048576 | tf_op jit(solution)/shard_map/all_to_all | solution.py:84
  16.7 18.7 %copy-start.11 = (s32[4,4]{1,0:T(4,128)S(1)}, s32[4,4]{1,0:T(4,128)}, u32[]{:S(2)}) copy-start(s32[4,4]{1,0:T(4,128)} %param.15) | copy-start | bytes 196
  31.2 17.5 %all-to-all-start = ((bf16[4,128,512]{2,1,0:T(8,128)(2,1)}), bf16[4,128,512]{2,1,0:T(8,128)(2,1)S(1)}, u32[]{:S(2)}, u32[]{:S(2)}) async-start(bf16[4,128,512]{2,1,0:T(8,128)(2,1)} %gather_fusion.3), calls=%async_computation | async-start | bytes 1048576 | tf_op jit(solution)/shard_map/all_to_all | solution.py:85
  34.6 341.0 %all-gather.3.cloned.1.call-start = ((), (), s32[]{:S(2)}) async-start(), calls=%async_computation.4 | async-start | bytes 20971520 | tf_op jit(solution)/shard_map/all_gather | solution.py:109
  36.1 0.8 copy-start.5
  49.2 0.8 copy-start.7
  65.2 3.9 copy-start.10
  65.2 5.4 copy-start.8
  65.2 6.3 %copy-start.6 = (bf16[4,128,512]{2,1,0:T(8,128)(2,1)S(1)}, bf16[4,128,512]{2,1,0:T(8,128)(2,1)}, u32[]{:S(2)}) copy-start(bf16[4,128,512]{2,1,0:T(8,128)(2,1)} %copy-done.5) | copy-start | bytes 1572868
  65.2 90.7 %all-to-all-start.2 = ((bf16[4,128,1536]{2,1,0:T(8,128)(2,1)}), bf16[4,128,1536]{2,1,0:T(8,128)(2,1)S(1)}, u32[]{:S(2)}, u32[]{:S(2)}) async-start(bf16[4,128,1536]{2,1,0:T(8,128)(2,1)} %gather_fusion.10), calls=%async_computation.2 | async-start | bytes 3145728 | tf_op jit(solution)/shard_map/all_to_all | solution.py:83
  400.5 3.1 copy-start.4
  406.6 4.6 copy-start.2
  411.2 1.6 copy-start.3
  429.5 3.1 copy-start.4
  435.6 4.6 copy-start.2
  440.1 1.6 copy-start.3
  458.4 3.1 copy-start.4
  464.5 4.6 copy-start.2
  469.1 1.6 copy-start.3
  487.4 3.1 copy-start.4
  493.5 4.6 copy-start.2
  498.1 1.6 copy-start.3
  517.1 41.0 %all-to-all-start.3 = ((bf16[4,128,1536]{2,1,0:T(8,128)(2,1)}), bf16[4,128,1536]{2,1,0:T(8,128)(2,1)S(1)}, u32[]{:S(2)}, u32[]{:S(2)}) async-start(bf16[4,128,1536]{2,1,0:T(8,128)(2,1)} %gather_fusion.14), calls=%async_computation.3 | async-start | bytes 3145728 | tf_op jit(solution)/shard_map/all_to_all | solution.py:123
  559.8 6.6 %copy-start.1 = (s32[16]{0:T(128)S(1)}, s32[16]{0:T(128)}, u32[]{:S(2)}) copy-start(s32[16]{0:T(128)} %param.14) | copy-start | bytes 196
Sparse Core Ops, SparseCore 0:
  56.8 318.7 all-gather.2
